TPU v7x, 128 devices: a whole 4x4x4 slice. The times are simulated.
128 devices in a mesh: slab: 16 (over z, x), pencil: 8 (over y, core).
Axes of the slice: x: 4, y: 4, z: 4, core: 2. Of those that a mesh axis runs over, the one named last changes fastest.
Arguments:
- a_blocks: float32 [256, 64, 20480], P('slab', 'pencil'), may hold values from -1 to 8, as said below
- col_codes: int32 [256, 64, 5], P('slab', 'pencil'), may hold values from 0 to 8, as said below
- agg_of: int32 [256, 64], P('slab', 'pencil'), may hold values from 0 to 2047, as said below
- test_vectors: float32 [256, 64, 2048], P('slab', 'pencil'), may hold values from -36 to 36
Outputs:
- relaxed: float32 [256, 64, 2048], P('slab', 'pencil')
- tiles: float32 [256, 64, 512], P('slab', 'pencil')
- products: float32 [256, 64, 2560], P('slab', 'pencil')
Inputs may be any that keep to these rules, and one draw needn't show every extreme that they name: `col_codes`: slot 0 of every block row is code 4, the block row itself; slots 1 to 4 hold different codes among the other eight of the 3 x 3 neighbourhood. `agg_of`: aggregate g is owned by device g // 16, devices numbered slab-major. On each device the block rows, in row-major order, form 64 groups of 2 consecutive block rows; all block rows of a group belong to aggregates of one owner, and the groups of one device go to different owners. Some owners receive a group from every device. `a_blocks`: the diagonal entries of every slot-0 block lie in [1.99, 8].
All inputs are finite; a program needn't handle non-finite values.
Results may differ from a plain program's by a relative error of at most 0.0003.
Values sent between devices are 32-bit elements; how exact they have to be, the bound alone decides.
A program may use at most 320 MiB of HBM per device.

v0:
```python
import math
import jax
import jax.numpy as jnp
from jax import lax
from jax.sharding import PartitionSpec as P

BLK = 64
NV = 32
NC = 8
KS = 5
ITERS = 2
OMEGA = 2.0 / 3.0
FULL_PRECISION = lax.Precision.HIGHEST


def with_halo(cells, sides, width):
    for axis, dim in sides:
        count = lax.axis_size(axis)
        ends = count - 1
        head = lax.slice_in_dim(cells, 0, width, axis=dim)
        tail = lax.slice_in_dim(cells, cells.shape[dim] - width, cells.shape[dim], axis=dim)
        cells = jnp.concatenate(
            [
                lax.ppermute(tail, axis, [(i, (i + 1) % count) for i in range(ends)]),
                cells,
                lax.ppermute(head, axis, [((i + 1) % count, i) for i in range(ends)]),
            ],
            axis=dim,
        )
    return cells


def coarse_modes(cells, coarse):
    centre = jnp.arange(cells, dtype=jnp.float32) + 0.5
    order = jnp.arange(coarse, dtype=jnp.float32)
    return jnp.cos(math.pi * centre[:, None] * order[None, :] / cells)


def solve_maps(coarse):
    gram = jnp.einsum("gkv,glv->gkl", coarse, coarse, precision=FULL_PRECISION)
    trace_sum = jnp.trace(gram, axis1=1, axis2=2)
    ridge = 0.1 * trace_sum / NC + 1e-06
    gram = gram + ridge[:, None, None] * jnp.eye(NC, dtype=jnp.float32)[None]
    lower = jnp.linalg.cholesky(gram)
    half_solved = jax.scipy.linalg.solve_triangular(lower, coarse, lower=True)
    solved = jax.scipy.linalg.solve_triangular(lower, half_solved, lower=True, trans=1)
    return jnp.swapaxes(solved, 1, 2)


def slot_index(col_codes):
    height, across_devices = (col_codes.shape[0], col_codes.shape[1])
    row_pos = jnp.arange(height, dtype=jnp.int32)[:, None, None] + col_codes // 3
    col_pos = jnp.arange(across_devices, dtype=jnp.int32)[None, :, None] + col_codes % 3
    return (row_pos * (across_devices + 2) + col_pos).reshape(-1)


def pick_rows(padded, flat_index, height, across_devices):
    features = padded.shape[2]
    flat = padded.reshape(padded.shape[0] * padded.shape[1], features)
    picked = jnp.take(flat, flat_index, axis=0)
    return picked.reshape(height, across_devices, KS, features)


def fit_slots(slot_coefficient, slot_ids, per_owner):
    members = (slot_ids[None, :] == jnp.arange(per_owner, dtype=jnp.int32)[:, None]).astype(
        jnp.float32
    )
    counts = jnp.sum(members, axis=1)
    summed = jnp.dot(
        members,
        slot_coefficient.reshape(slot_coefficient.shape[0], NC * NV),
        precision=FULL_PRECISION,
    )
    coarse = summed.reshape(per_owner, NC, NV) / jnp.maximum(counts, 1.0)[:, None, None]
    maps = solve_maps(coarse)
    return jnp.dot(members.T, maps.reshape(per_owner, NV * NC), precision=FULL_PRECISION)


def pack_slots(chosen_f, payload, group_list, capacity):
    flat = payload.reshape(group_list, capacity * payload.shape[1])
    packed = jnp.dot(chosen_f, flat, precision=FULL_PRECISION)
    return packed.reshape(chosen_f.shape[0], capacity, payload.shape[1])


def unpack_slots(chosen_f, received, block_rows):
    flat = received.reshape(received.shape[0], received.shape[1] * received.shape[2])
    return jnp.dot(chosen_f.T, flat, precision=FULL_PRECISION).reshape(
        block_rows, received.shape[2]
    )


def send_owner(payload, slot_ids):
    arrived, arrived_ids = (
        lax.all_to_all(payload, ("slab", "pencil"), split_axis=0, concat_axis=0, tiled=True),
        lax.all_to_all(slot_ids, ("slab", "pencil"), split_axis=0, concat_axis=0, tiled=True),
    )
    return (arrived, arrived_ids)


def send_back(payload):
    returned = lax.all_to_all(payload, ("slab", "pencil"), split_axis=0, concat_axis=0, tiled=True)
    return returned


def shards(a_blocks, col_codes, agg_of, test_vectors):
    height, across_devices = (agg_of.shape[0], agg_of.shape[1])
    n_slab = lax.axis_size("slab")
    n_pencil = lax.axis_size("pencil")
    devices = n_slab * n_pencil
    blocks = a_blocks.reshape(height, across_devices, KS, BLK, BLK)
    diagonal = jnp.diagonal(blocks[:, :, 0], axis1=-2, axis2=-1)
    block_wide = jnp.transpose(blocks, (0, 1, 3, 2, 4)).reshape(
        height, across_devices, BLK, KS * BLK
    )
    flat_index = slot_index(col_codes)
    candidate_vectors = test_vectors.reshape(height, across_devices, BLK, NV)
    for sweep in range(ITERS):
        padded = with_halo(
            candidate_vectors.reshape(height, across_devices, BLK * NV),
            (("slab", 0), ("pencil", 1)),
            1,
        )
        picked = pick_rows(padded, flat_index, height, across_devices).reshape(
            height, across_devices, KS * BLK, NV
        )
        image = jnp.einsum("ijor,ijrw->ijow", block_wide, picked, precision=FULL_PRECISION)
        candidate_vectors = candidate_vectors - OMEGA * image / diagonal[:, :, :, None]
    squares = jnp.sum(candidate_vectors * candidate_vectors, axis=(0, 1, 2))
    totals = lax.psum(squares, ("slab", "pencil"))
    scale = jnp.sqrt(totals / (height * across_devices * BLK * devices) + 1e-06)
    relaxed = candidate_vectors / scale
    block_rows = height * across_devices
    capacity = 2 * block_rows // devices
    group_list = devices // 2
    per_owner = block_rows // 8
    near_null_modes = coarse_modes(BLK, NC)
    row_vectors = relaxed.reshape(block_rows, BLK, NV)
    group_agg = agg_of.reshape(group_list, capacity)
    group_owner = group_agg[:, 0] // per_owner
    chosen = group_owner[None, :] == jnp.arange(devices, dtype=jnp.int32)[:, None]
    chosen_f = chosen.astype(jnp.float32)
    slot_ids = (
        jnp.sum(jnp.where(chosen[:, :, None], group_agg[None] % per_owner + 1, 0), axis=1) - 1
    )
    slot_count = devices * capacity
    outgoing = pack_slots(chosen_f, row_vectors.reshape(block_rows, BLK * NV), group_list, capacity)
    arrived, arrived_ids = send_owner(outgoing, slot_ids)
    slot_vector_rows = arrived.reshape(slot_count, BLK, NV)
    slot_coefficient = jnp.einsum(
        "wd,xwf->xdf", near_null_modes, slot_vector_rows, precision=FULL_PRECISION
    )
    slot_maps = fit_slots(slot_coefficient, arrived_ids.reshape(slot_count), per_owner)
    slot_tiles = jnp.einsum(
        "scv,svk->sck",
        slot_vector_rows,
        slot_maps.reshape(slot_count, NV, NC),
        precision=FULL_PRECISION,
    )
    returned = send_back(slot_tiles.reshape(devices, capacity, BLK * NC))
    tile_rows = unpack_slots(chosen_f, returned, block_rows).reshape(block_rows, BLK, NC)
    tile_grid = tile_rows.reshape(height, across_devices, BLK * NC)
    padded_tiles = with_halo(tile_grid, (("slab", 0), ("pencil", 1)), 1)
    picked_tiles = pick_rows(padded_tiles, flat_index, height, across_devices).reshape(
        height, across_devices, KS, BLK, NC
    )
    products = jnp.einsum("ijkoc,ijkcw->ijkow", blocks, picked_tiles, precision=FULL_PRECISION)
    return (
        relaxed.reshape(height, across_devices, BLK * NV),
        tile_grid,
        products.reshape(height, across_devices, KS * BLK * NC),
    )


def solution(mesh):
    in_specs = (
        P("slab", "pencil", None),
        P("slab", "pencil", None),
        P("slab", "pencil"),
        P("slab", "pencil", None),
    )
    out_specs = (P("slab", "pencil", None), P("slab", "pencil", None), P("slab", "pencil", None))
    return jax.shard_map(shards, mesh=mesh, in_specs=in_specs, out_specs=out_specs, check_vma=False)
```

profile of v0, /device:TPU:7, one launch (start us, length us, event | category | flops | bytes accessed | tf_op | source)
XLA Modules:
  0.0 639.7 jit_solution(15918062208513373529)
XLA Ops:
  1.6 2.5 collective-permute-start.1
  4.1 4.9 collective-permute-start
  11.9 38.9 %copy.177 = f32[16,8,20480]{0,1,2:T(8,128)} copy(f32[16,8,20480]{2,1,0:T(8,128)} %param.6) | data formatting | bytes 20971520 | tf_op args[0]
  50.9 11.6 %slice_bitcast_fusion = f32[16,8,64,64]{0,1,3,2:T(8,128)} fusion(f32[16,8,5,64,64]{0,1,4,3,2:T(8,128)} %bitcast), kind=kLoop, calls=%fused_computation.6 | loop fusion | bytes 4194304 | tf_op jit(solution)/shard_map/squeeze | solution.py:111
  63.2 4.3 collective-permute-start.2
  69.5 2.7 reshape.237
  72.2 3.8 copy.182
  76.0 6.4 %gather_fusion = f32[64,16,8]{1,2,0:T(8,128)S(1)} fusion(f32[16,8,64,64]{0,1,3,2:T(8,128)} %slice_bitcast_fusion, s32[64]{0:T(128)S(1)} %or_bitcast_fusion), kind=kCustom, calls=%fused_computation.2 | custom fusion | bytes 66048 | tf_op jit(solution)/shard_map/jit(diagonal)/gather | solution.py:111
  82.6 63.1 %copy.178 = f32[16,8,64,5,64]{2,4,3,1,0:T(8,128)} copy(f32[16,8,64,5,64]{0,1,4,2,3:T(8,128)} %bitcast.1) | data formatting | bytes 20971520 | tf_op jit(solution)/shard_map/transpose | solution.py:112
  146.0 2.3 copy.176
  150.0 4.6 gather_fusion.2
  154.6 5.2 broadcast_select_fusion.1
  159.8 13.7 %reshape_reshape.7 = f32[16,8,320,32]{3,2,1,0:T(8,128)} reshape(f32[640,2048]{1,0:T(8,128)} %broadcast_select_fusion.1) | data formatting | bytes 10485760 | tf_op jit(solution)/shard_map/reshape;reshape | solution.py:123
  173.5 37.9 %bitcast_subtract_fusion.1 = f32[16,8,64,32]{2,3,1,0:T(8,128)S(1)} fusion(f32[16,8,64,32]{2,3,1,0:T(8,128)} %copy.182, f32[16,8,320,32]{3,2,1,0:T(8,128)} %reshape_reshape.7, f32[16,8,64,320]{2,3,1,0:T(8,128)} %bitcast.82, f32[16,8,64]{2,1,0:T(8,128)S(1)} %copy.181), kind=kOutput, calls=%fused_computation.13 | convolution fusion | flops 1007419392 | bytes 17858560 | tf_op jit(solution)/shard_map/ijor,ijrw->ijow/dot_general | solution.py:126
  213.7 2.8 copy.184
  216.8 3.4 collective-permute-start.5
  220.2 3.6 reshape.242
  224.2 4.7 collective-permute-start.6
  231.6 10.5 %all-to-all-start.1 = ((s32[128,1,2]{2,1,0:T(1,128)}), s32[128,1,2]{2,1,0:T(1,128)S(1)}, u32[]{:S(2)}, u32[]{:S(2)}) async-start(s32[128,1,2]{2,1,0:T(1,128)} %copy.196), calls=%async_computation.1 | async-start | bytes 131072 | tf_op jit(solution)/shard_map/all_to_all | solution.py:95
  245.7 4.6 gather_fusion.3
  250.2 5.2 broadcast_select_fusion
  255.5 13.8 %reshape_reshape.8 = f32[16,8,320,32]{3,2,1,0:T(8,128)} reshape(f32[640,2048]{1,0:T(8,128)} %broadcast_select_fusion) | data formatting | bytes 10485760 | tf_op jit(solution)/shard_map/reshape;reshape | solution.py:123
  269.3 38.3 %multiply_reduce_fusion = (f32[32]{0:T(128)S(1)}, f32[16,8,64,32]{2,3,1,0:T(8,128)}) fusion(f32[16,8,64,32]{2,3,1,0:T(8,128)S(1)} %copy-done.1, f32[16,8,64]{2,1,0:T(8,128)S(1)} %copy.181, f32[16,8,320,32]{3,2,1,0:T(8,128)} %reshape_reshape.8, f32[16,8,64,320]{2,3,1,0:T(8,128)} %bitcast.83), kind=kOutput, calls=%fused_computation.14 | convolution fusion | flops 1007943680 | bytes 17858688 | tf_op jit(solution)/shard_map/ijor,ijrw->ijow/dot_general | solution.py:126
  307.6 65.2 %psum.7 = f32[32]{0:T(128)S(1)} all-reduce(f32[32]{0:T(128)S(1)} %get-tuple-element.33), channel_id=1, replica_groups=mesh['slab'=16,'pencil'=8] {'slab','pencil'}, use_global_device_ids=true, to_apply=%region_1.3 | all-reduce | flops 32 | bytes 256 | tf_op jit(solution)/shard_map/psum | solution.py:129
  374.8 2.8 copy.188
  377.6 3.5 reshape_reshape_reshape.6
  382.3 2.9 copy.192
  385.2 7.3 %all-to-all-start = ((f32[128,2,2048]{2,1,0:T(2,128)}), f32[128,2,2048]{2,1,0:T(2,128)S(1)}, u32[]{:S(2)}, u32[]{:S(2)}) async-start(f32[128,2,2048]{2,1,0:T(2,128)} %copy.192), calls=%async_computation | async-start | bytes 4194304 | tf_op jit(solution)/shard_map/all_to_all | solution.py:94
  394.1 26.8 %all-to-all-done = f32[128,2,2048]{2,1,0:T(2,128)S(1)} async-done(((f32[128,2,2048]{2,1,0:T(2,128)}), f32[128,2,2048]{2,1,0:T(2,128)S(1)}, u32[]{:S(2)}, u32[]{:S(2)}) %all-to-all-start) | async-done | bytes 2097184 | tf_op jit(solution)/shard_map/all_to_all | solution.py:94
  421.0 5.3 reshape.246
  426.3 7.0 %copy.197 = f32[256,64,32]{0,1,2:T(8,128)S(1)} copy(f32[256,64,32]{2,1,0:T(8,128)} %reshape.246) | data formatting | bytes 4194304 | tf_op jit(solution)/shard_map/reshape | solution.py:148
  435.6 11.7 %custom-call.11 = f32[16,8,8]{2,1,0:T(8,128)S(1)} custom-call(f32[16,8,8]{2,1,0:T(8,128)S(1)} %fusion.18), custom_call_target="Cholesky" | custom-call | tf_op jit(solution)/shard_map/jit(cholesky)/cholesky | solution.py:44
  447.6 10.0 %custom-call.12 = f32[16,1,8,8]{2,3,1,0:T(8,128)S(1)} custom-call(f32[16,1,8,8]{3,2,1,0:T(8,128)S(1)} %select_bitcast_fusion), custom_call_target="InvertDiagBlocksLowerTriangular" | custom-call | tf_op jit(solution)/shard_map/jit(_solve_triangular)/vmap()/triangular_solve | solution.py:46
  459.0 11.2 %fusion.56 = f32[256,64,8]{2,1,0:T(8,128)} fusion(f32[256,64,32]{2,1,0:T(8,128)} %reshape.246, f32[256,32,8]{1,2,0:T(8,128)S(1)} %copy.209), kind=kOutput, calls=%fused_computation.114 | convolution fusion | flops 50331648 | bytes 2883584 | tf_op jit(solution)/shard_map/scv,svk->sck/dot_general | solution.py:153
  470.2 7.4 %reshape.249 = f32[128,2,512]{2,1,0:T(2,128)} reshape(f32[256,64,8]{2,1,0:T(8,128)} %fusion.56) | data formatting | bytes 1048576 | tf_op jit(solution)/shard_map/reshape | solution.py:159
  477.6 6.3 all-to-all-start.2
  484.1 11.8 %all-to-all-done.2 = f32[128,2,512]{2,1,0:T(2,128)S(1)} async-done(((f32[128,2,512]{2,1,0:T(2,128)}), f32[128,2,512]{2,1,0:T(2,128)S(1)}, u32[]{:S(2)}, u32[]{:S(2)}) %all-to-all-start.2) | async-done | bytes 524320 | tf_op jit(solution)/shard_map/all_to_all | solution.py:101
  496.3 3.8 collective-permute-start.8
  502.2 4.6 collective-permute-done.9
  506.8 3.1 collective-permute-start.10
  509.9 2.7 collective-permute-start.11
  512.7 55.6 %copy.214 = f32[16,8,5,64,64]{4,3,2,1,0:T(8,128)} copy(f32[16,8,5,64,64]{0,1,4,3,2:T(8,128)} %bitcast) | data formatting | bytes 20971520 | tf_op jit(solution)/shard_map/reshape | solution.py:110
  568.4 4.5 reshape.244
  573.1 2.2 gather_fusion.1
  575.2 13.6 %gather.15 = f32[16,8,5,64,8]{4,3,2,1,0:T(8,128)} reshape(f32[640,512]{1,0:T(8,128)S(1)} %gather_fusion.1) | data formatting | bytes 2621440 | tf_op jit(solution)/shard_map/jit(_take)/gather | solution.py:60
  588.8 37.9 %fusion.4 = f32[16,8,5,64,8]{3,4,2,1,0:T(8,128)S(1)} fusion(f32[16,8,5,64,64]{4,3,2,1,0:T(8,128)} %copy.214, f32[16,8,5,64,8]{4,3,2,1,0:T(8,128)} %gather.15, pred[16,8,5]{2,1,0:T(8,128)(4,1)S(1)} %copy.211), kind=kOutput, calls=%fused_computation.16 | convolution fusion | flops 251985920 | bytes 13107840 | tf_op jit(solution)/shard_map/ijkoc,ijkcw->ijkow/dot_general | solution.py:166
  626.7 6.0 copy.215
  632.7 6.8 %copy.216 = f32[16,8,2560]{2,1,0:T(8,128)} copy(f32[16,8,2560]{0,2,1:T(8,128)} %bitcast.84) | data formatting | bytes 2621440
  (112 shorter events, 29.2 us)
Async XLA Ops:
  1.6 61.6 %collective-permute-start.1 = (f32[1,8,2048]{2,0,1:T(1,128)S(1)}, f32[1,8,2048]{2,0,1:T(1,128)S(1)}, u32[]{:S(2)}, u32[]{:S(2)}) collective-permute-start(f32[1,8,2048]{2,0,1:T(1,128)S(1)} %copy.174), channel_id=1, source_target_pairs={{8,0},{16,8},{24,16},{32,24},{40,32},{48,40},{56,48},{64,56},{72,6... | collective-permute-start | bytes 196616 | tf_op jit(solution)/shard_map/ppermute | solution.py:26
  4.1 59.0 %collective-permute-start = (f32[1,8,2048]{2,0,1:T(1,128)S(1)}, f32[1,8,2048]{2,0,1:T(1,128)S(1)}, u32[]{:S(2)}, u32[]{:S(2)}) collective-permute-start(f32[1,8,2048]{2,0,1:T(1,128)S(1)} %copy.173), channel_id=1, source_target_pairs={{0,8},{8,16},{16,24},{24,32},{32,40},{40,48},{48,56},{56,64},{64,7... | collective-permute-start | bytes 196616 | tf_op jit(solution)/shard_map/ppermute | solution.py:24
  11.6 39.3 %copy-start.4 = (s32[16,8,5]{2,1,0:T(8,128)}, s32[16,8,5]{2,1,0:T(8,128)S(1)}, u32[]{:S(2)}) copy-start(s32[16,8,5]{2,1,0:T(8,128)S(1)} %copy.172) | copy-start | bytes 7684
  11.9 39.0 %copy-start.7 = (s32[64]{0:T(128)}, s32[64]{0:T(128)S(1)}, u32[]{:S(2)}) copy-start(s32[64]{0:T(128)S(1)} %and_select_fusion.1) | copy-start | bytes 772
  50.9 11.7 %copy-start.2 = (f32[16,8,2048]{2,1,0:T(8,128)S(1)}, f32[16,8,2048]{2,1,0:T(8,128)}, u32[]{:S(2)}) copy-start(f32[16,8,2048]{2,1,0:T(8,128)} %param.9) | copy-start | bytes 3145732
  63.2 82.5 %collective-permute-start.2 = (f32[18,1,2048]{2,0,1:T(8,128)S(1)}, f32[18,1,2048]{2,0,1:T(8,128)S(1)}, u32[]{:S(2)}, u32[]{:S(2)}) collective-permute-start(f32[18,1,2048]{2,0,1:T(8,128)S(1)} %get-tuple-element.25), channel_id=1, source_target_pairs={{0,1},{1,2},{2,3},{3,4},{4,5},{5,6},{6,7},{8,9},{9,10},{10,11},{11... | collective-permute-start | bytes 442376 | tf_op jit(solution)/shard_map/ppermute | solution.py:24
  67.6 78.2 %collective-permute-start.3 = (f32[18,1,2048]{2,0,1:T(8,128)S(1)}, f32[18,1,2048]{2,0,1:T(8,128)S(1)}, u32[]{:S(2)}, u32[]{:S(2)}) collective-permute-start(f32[18,1,2048]{2,0,1:T(8,128)S(1)} %get-tuple-element.26), channel_id=1, source_target_pairs={{1,0},{2,1},{3,2},{4,3},{5,4},{6,5},{7,6},{9,8},{10,9},{11,10},{12... | collective-permute-start | bytes 442376 | tf_op jit(solution)/shard_map/ppermute | solution.py:26
  211.4 5.2 copy-start
  211.7 12.2 %collective-permute-start.4 = (f32[1,8,2048]{2,1,0:T(8,128)S(1)}, f32[1,8,2048]{2,1,0:T(8,128)S(1)}, u32[]{:S(2)}, u32[]{:S(2)}) collective-permute-start(f32[1,8,2048]{2,1,0:T(8,128)S(1)} %slice.78), channel_id=1, source_target_pairs={{0,8},{8,16},{16,24},{24,32},{32,40},{40,48},{48,56},{56,64},{64,7... | collective-permute-start | bytes 196616 | tf_op jit(solution)/shard_map/ppermute | solution.py:24
  216.8 7.1 %collective-permute-start.5 = (f32[1,8,2048]{2,1,0:T(8,128)S(1)}, f32[1,8,2048]{2,1,0:T(8,128)S(1)}, u32[]{:S(2)}, u32[]{:S(2)}) collective-permute-start(f32[1,8,2048]{2,1,0:T(8,128)S(1)} %slice.80), channel_id=1, source_target_pairs={{8,0},{16,8},{24,16},{32,24},{40,32},{48,40},{56,48},{64,56},{72,6... | collective-permute-start | bytes 196616 | tf_op jit(solution)/shard_map/ppermute | solution.py:26
  224.2 18.0 %collective-permute-start.6 = (f32[18,1,2048]{2,1,0:T(1,128)S(1)}, f32[18,1,2048]{2,1,0:T(1,128)S(1)}, u32[]{:S(2)}, u32[]{:S(2)}) collective-permute-start(f32[18,1,2048]{2,1,0:T(1,128)S(1)} %get-tuple-element.23), channel_id=1, source_target_pairs={{0,1},{1,2},{2,3},{3,4},{4,5},{5,6},{6,7},{8,9},{9,10},{10,11},{11... | collective-permute-start | bytes 442376 | tf_op jit(solution)/shard_map/ppermute | solution.py:24
  228.9 13.2 %collective-permute-start.7 = (f32[18,1,2048]{2,1,0:T(1,128)S(1)}, f32[18,1,2048]{2,1,0:T(1,128)S(1)}, u32[]{:S(2)}, u32[]{:S(2)}) collective-permute-start(f32[18,1,2048]{2,1,0:T(1,128)S(1)} %get-tuple-element.24), channel_id=1, source_target_pairs={{1,0},{2,1},{3,2},{4,3},{5,4},{6,5},{7,6},{9,8},{10,9},{11,10},{12... | collective-permute-start | bytes 442376 | tf_op jit(solution)/shard_map/ppermute | solution.py:26
  231.6 153.6 %all-to-all-start.1 = ((s32[128,1,2]{2,1,0:T(1,128)}), s32[128,1,2]{2,1,0:T(1,128)S(1)}, u32[]{:S(2)}, u32[]{:S(2)}) async-start(s32[128,1,2]{2,1,0:T(1,128)} %copy.196), calls=%async_computation.1 | async-start | bytes 131072 | tf_op jit(solution)/shard_map/all_to_all | solution.py:95
  255.5 13.8 %copy-start.1 = (f32[16,8,64,32]{2,3,1,0:T(8,128)S(1)}, f32[16,8,64,32]{2,3,1,0:T(8,128)}, u32[]{:S(2)}) copy-start(f32[16,8,64,32]{2,3,1,0:T(8,128)} %copy-done) | copy-start | bytes 3145732
  377.6 3.5 copy-start.8
  385.2 35.8 %all-to-all-start = ((f32[128,2,2048]{2,1,0:T(2,128)}), f32[128,2,2048]{2,1,0:T(2,128)S(1)}, u32[]{:S(2)}, u32[]{:S(2)}) async-start(f32[128,2,2048]{2,1,0:T(2,128)} %copy.192), calls=%async_computation | async-start | bytes 4194304 | tf_op jit(solution)/shard_map/all_to_all | solution.py:94
  470.2 13.7 %copy-start.5 = (s32[16,8,5]{2,1,0:T(8,128)S(1)}, s32[16,8,5]{2,1,0:T(8,128)}, u32[]{:S(2)}) copy-start(s32[16,8,5]{2,1,0:T(8,128)} %copy-done.4) | copy-start | bytes 7684
  477.6 18.3 %all-to-all-start.2 = ((f32[128,2,512]{2,1,0:T(2,128)}), f32[128,2,512]{2,1,0:T(2,128)S(1)}, u32[]{:S(2)}, u32[]{:S(2)}) async-start(f32[128,2,512]{2,1,0:T(2,128)} %reshape.249), calls=%async_computation.2 | async-start | bytes 1048576 | tf_op jit(solution)/shard_map/all_to_all | solution.py:101
  496.3 5.8 collective-permute-start.8
  500.1 68.1 %copy-start.3 = (f32[16,8,512]{2,1,0:T(8,128)}, f32[16,8,512]{2,1,0:T(8,128)S(1)}, u32[]{:S(2)}) copy-start(f32[16,8,512]{2,1,0:T(8,128)S(1)} %reshape_reshape_reshape.7) | copy-start | bytes 786436
  500.2 6.6 %collective-permute-start.9 = (f32[1,8,512]{2,1,0:T(8,128)S(1)}, f32[1,8,512]{2,1,0:T(8,128)S(1)}, u32[]{:S(2)}, u32[]{:S(2)}) collective-permute-start(f32[1,8,512]{2,1,0:T(8,128)S(1)} %slice.87), channel_id=1, source_target_pairs={{8,0},{16,8},{24,16},{32,24},{40,32},{48,40},{56,48},{64,56},{72,6... | collective-permute-start | bytes 49160 | tf_op jit(solution)/shard_map/ppermute | solution.py:26
  506.8 66.1 %collective-permute-start.10 = (f32[18,1,512]{2,1,0:T(1,128)S(1)}, f32[18,1,512]{2,1,0:T(1,128)S(1)}, u32[]{:S(2)}, u32[]{:S(2)}) collective-permute-start(f32[18,1,512]{2,1,0:T(1,128)S(1)} %get-tuple-element.29), channel_id=1, source_target_pairs={{0,1},{1,2},{2,3},{3,4},{4,5},{5,6},{6,7},{8,9},{9,10},{10,11},{11... | collective-permute-start | bytes 110600 | tf_op jit(solution)/shard_map/ppermute | solution.py:24
  509.9 63.0 %collective-permute-start.11 = (f32[18,1,512]{2,1,0:T(1,128)S(1)}, f32[18,1,512]{2,1,0:T(1,128)S(1)}, u32[]{:S(2)}, u32[]{:S(2)}) collective-permute-start(f32[18,1,512]{2,1,0:T(1,128)S(1)} %get-tuple-element.30), channel_id=1, source_target_pairs={{1,0},{2,1},{3,2},{4,3},{5,4},{6,5},{7,6},{9,8},{10,9},{11,10},{12... | collective-permute-start | bytes 110600 | tf_op jit(solution)/shard_map/ppermute | solution.py:26
  512.7 55.6 %copy-start.6 = (pred[16,8,5]{0,1,2:T(8,128)(4,1)S(1)}, pred[16,8,5]{0,1,2:T(8,128)(4,1)}, u32[]{:S(2)}) copy-start(pred[16,8,5]{0,1,2:T(8,128)(4,1)} %get-tuple-element.19) | copy-start | bytes 1924
where the time goes:
time: 651 us; the launch traced here: 640 us
  local copies, waits for them, and re-layouts  300 us (46%)
  matrix products  130 us (20%)
  blocking collectives  65.2 us (10%)
  starting transfers between devices  61.2 us (9%)
  waiting for transfers between devices  43.2 us (7%)
  other arithmetic  39.2 us (6%)
    dot_general x2, matrix products, shards(): jnp.einsum('ijor,ijrw->ijow', block_wide, picked, precision=FULL_PRECISION)  76.2 us
    psum x1, blocking collectives, shards(): totals = lax.psum(squares, ('slab', 'pencil'))  65.2 us
    transpose x1, local copies, waits for them, and re-layouts, shards(): jnp.transpose(blocks, (0, 1, 3, 2, 4))  63.1 us
    reshape x1, local copies, waits for them, and re-layouts, shards(): blocks = a_blocks.reshape(height, across_devices, KS, BLK, BLK)  55.6 us
    unnamed x27, local copies, waits for them, and re-layouts  47.3 us
    dot_general x1, matrix products, shards(): jnp.einsum('ijkoc,ijkcw->ijkow', blocks, picked_tiles, precision=FULL_PRE...  37.9 us
    another operation x2, local copies, waits for them, and re-layouts, shards(): pick_rows(padded, flat_index, height, across_devices)  27.5 us
    all_to_all x1, waiting for transfers between devices, send_owner(): lax.all_to_all(payload, ('slab', 'pencil'), split_axis=0, concat_axis=0,...  26.8 us
  transfers between devices with their start and end apart: 15, of which 3 were waited for; matrix products, arithmetic and copies ran while one was open for 43% of the time, Pallas kernels for 0%

commit v1 on v0

--- a/solution.py
+++ b/solution.py
@@ -126,7 +126,8 @@
         image = jnp.einsum("ijor,ijrw->ijow", block_wide, picked, precision=FULL_PRECISION)
         candidate_vectors = candidate_vectors - OMEGA * image / diagonal[:, :, :, None]
     squares = jnp.sum(candidate_vectors * candidate_vectors, axis=(0, 1, 2))
-    totals = lax.psum(squares, ("slab", "pencil"))
+    piece_next = lax.psum(squares, "slab")
+    totals = lax.psum(piece_next, "pencil")
     scale = jnp.sqrt(totals / (height * across_devices * BLK * devices) + 1e-06)
     relaxed = candidate_vectors / scale
     block_rows = height * across_devices

time: 651 us -> 636 us (0.977)
  blocking collectives: 65.2 us -> 45.2 us
    psum x1 -> x2, blocking collectives: 65.2 us -> 45.2 us  [the longest x1 25.8 us: shards(): piece_next = lax.psum(squares, 'slab')]
  transfers between devices with their start and end apart: 15 -> 15, of which waited for: 3 -> 3; matrix products, arithmetic and copies ran while one was open for 43% -> 44% of each run, Pallas kernels for 0% -> 0%
where the time goes in v1:
time: 636 us; the launch traced here: 625 us
  local copies, waits for them, and re-layouts  300 us (47%)
  matrix products  129 us (20%)
  starting transfers between devices  66.6 us (10%)
  blocking collectives  45.2 us (7%)
  waiting for transfers between devices  43.3 us (7%)
  other arithmetic  39.3 us (6%)
    dot_general x2, matrix products, shards(): jnp.einsum('ijor,ijrw->ijow', block_wide, picked, precision=FULL_PRECISION)  75.9 us
    transpose x1, local copies, waits for them, and re-layouts, shards(): jnp.transpose(blocks, (0, 1, 3, 2, 4))  63.1 us
    reshape x1, local copies, waits for them, and re-layouts, shards(): blocks = a_blocks.reshape(height, across_devices, KS, BLK, BLK)  55.7 us
    unnamed x27, local copies, waits for them, and re-layouts  47.3 us
    dot_general x1, matrix products, shards(): jnp.einsum('ijkoc,ijkcw->ijkow', blocks, picked_tiles, precision=FULL_PRE...  37.9 us
    another operation x2, local copies, waits for them, and re-layouts, shards(): pick_rows(padded, flat_index, height, across_devices)  27.5 us
    all_to_all x1, waiting for transfers between devices, send_owner(): lax.all_to_all(payload, ('slab', 'pencil'), split_axis=0, concat_axis=0,...  26.9 us
    psum x1, blocking collectives, shards(): piece_next = lax.psum(squares, 'slab')  25.8 us
  transfers between devices with their start and end apart: 15, of which 3 were waited for; matrix products, arithmetic and copies ran while one was open for 44% of the time, Pallas kernels for 0%

profile of v1, /device:TPU:7, one launch (start us, length us, event | category | flops | bytes accessed | tf_op | source)
XLA Modules:
  0.0 625.1 jit_solution(5671844948510901150)
XLA Ops:
  1.6 2.5 collective-permute-start.1
  4.1 4.9 collective-permute-start
  11.9 38.9 %copy.177 = f32[16,8,20480]{0,1,2:T(8,128)} copy(f32[16,8,20480]{2,1,0:T(8,128)} %param.6) | data formatting | bytes 20971520 | tf_op args[0]
  50.9 11.6 %slice_bitcast_fusion = f32[16,8,64,64]{0,1,3,2:T(8,128)} fusion(f32[16,8,5,64,64]{0,1,4,3,2:T(8,128)} %bitcast), kind=kLoop, calls=%fused_computation.6 | loop fusion | bytes 4194304 | tf_op jit(solution)/shard_map/squeeze | solution.py:111
  63.2 4.3 collective-permute-start.2
  69.5 2.7 reshape.237
  72.2 3.8 copy.182
  76.0 6.4 %gather_fusion = f32[64,16,8]{1,2,0:T(8,128)S(1)} fusion(f32[16,8,64,64]{0,1,3,2:T(8,128)} %slice_bitcast_fusion, s32[64]{0:T(128)S(1)} %or_bitcast_fusion), kind=kCustom, calls=%fused_computation.2 | custom fusion | bytes 66048 | tf_op jit(solution)/shard_map/jit(diagonal)/gather | solution.py:111
  82.6 63.1 %copy.178 = f32[16,8,64,5,64]{2,4,3,1,0:T(8,128)} copy(f32[16,8,64,5,64]{0,1,4,2,3:T(8,128)} %bitcast.1) | data formatting | bytes 20971520 | tf_op jit(solution)/shard_map/transpose | solution.py:112
  146.1 2.3 copy.176
  150.0 4.6 gather_fusion.2
  154.6 5.2 broadcast_select_fusion.1
  159.8 13.7 %reshape_reshape.7 = f32[16,8,320,32]{3,2,1,0:T(8,128)} reshape(f32[640,2048]{1,0:T(8,128)} %broadcast_select_fusion.1) | data formatting | bytes 10485760 | tf_op jit(solution)/shard_map/reshape;reshape | solution.py:123
  173.5 37.6 %bitcast_subtract_fusion.1 = f32[16,8,64,32]{2,3,1,0:T(8,128)S(1)} fusion(f32[16,8,64,32]{2,3,1,0:T(8,128)} %copy.182, f32[16,8,320,32]{3,2,1,0:T(8,128)} %reshape_reshape.7, f32[16,8,64,320]{2,3,1,0:T(8,128)} %bitcast.82, f32[16,8,64]{2,1,0:T(8,128)S(1)} %copy.181), kind=kOutput, calls=%fused_computation.13 | convolution fusion | flops 1007419392 | bytes 17858560 | tf_op jit(solution)/shard_map/ijor,ijrw->ijow/dot_general | solution.py:126
  213.4 2.8 copy.184
  216.5 3.4 collective-permute-start.5
  219.9 3.6 reshape.242
  223.9 4.7 collective-permute-start.6
  231.3 10.8 %all-to-all-start.1 = ((s32[128,1,2]{2,1,0:T(1,128)}), s32[128,1,2]{2,1,0:T(1,128)S(1)}, u32[]{:S(2)}, u32[]{:S(2)}) async-start(s32[128,1,2]{2,1,0:T(1,128)} %copy.196), calls=%async_computation.1 | async-start | bytes 131072 | tf_op jit(solution)/shard_map/all_to_all | solution.py:95
  245.6 4.6 gather_fusion.3
  250.2 5.2 broadcast_select_fusion
  255.4 13.8 %reshape_reshape.8 = f32[16,8,320,32]{3,2,1,0:T(8,128)} reshape(f32[640,2048]{1,0:T(8,128)} %broadcast_select_fusion) | data formatting | bytes 10485760 | tf_op jit(solution)/shard_map/reshape;reshape | solution.py:123
  269.2 38.3 %multiply_reduce_fusion = (f32[32]{0:T(128)S(1)}, f32[16,8,64,32]{2,3,1,0:T(8,128)}) fusion(f32[16,8,64,32]{2,3,1,0:T(8,128)S(1)} %copy-done.1, f32[16,8,64]{2,1,0:T(8,128)S(1)} %copy.181, f32[16,8,320,32]{3,2,1,0:T(8,128)} %reshape_reshape.8, f32[16,8,64,320]{2,3,1,0:T(8,128)} %bitcast.83), kind=kOutput, calls=%fused_computation.14 | convolution fusion | flops 1007943680 | bytes 17858688 | tf_op jit(solution)/shard_map/ijor,ijrw->ijow/dot_general | solution.py:126
  307.5 25.8 %psum.14 = f32[32]{0:T(128)S(1)} all-reduce(f32[32]{0:T(128)S(1)} %get-tuple-element.33), channel_id=1, replica_groups=mesh['slab'=16,'pencil'=8] {'slab'}, use_global_device_ids=true, to_apply=%region_1.3 | all-reduce | flops 32 | bytes 256 | tf_op jit(solution)/shard_map/psum | solution.py:129
  333.3 19.4 %psum.15 = f32[32]{0:T(128)S(1)} all-reduce(f32[32]{0:T(128)S(1)} %psum.14), channel_id=1, replica_groups=mesh['slab'=16,'pencil'=8] {'pencil'}, use_global_device_ids=true, to_apply=%region_2.4 | all-reduce | flops 32 | bytes 256 | tf_op jit(solution)/shard_map/psum | solution.py:130
  354.8 2.8 copy.188
  357.6 3.5 reshape_reshape_reshape.6
  362.3 2.9 copy.192
  365.2 12.5 %all-to-all-start = ((f32[128,2,2048]{2,1,0:T(2,128)}), f32[128,2,2048]{2,1,0:T(2,128)S(1)}, u32[]{:S(2)}, u32[]{:S(2)}) async-start(f32[128,2,2048]{2,1,0:T(2,128)} %copy.192), calls=%async_computation | async-start | bytes 4194304 | tf_op jit(solution)/shard_map/all_to_all | solution.py:94
  379.3 26.9 %all-to-all-done = f32[128,2,2048]{2,1,0:T(2,128)S(1)} async-done(((f32[128,2,2048]{2,1,0:T(2,128)}), f32[128,2,2048]{2,1,0:T(2,128)S(1)}, u32[]{:S(2)}, u32[]{:S(2)}) %all-to-all-start) | async-done | bytes 2097184 | tf_op jit(solution)/shard_map/all_to_all | solution.py:94
  406.2 5.3 reshape.246
  411.6 7.0 %copy.197 = f32[256,64,32]{0,1,2:T(8,128)S(1)} copy(f32[256,64,32]{2,1,0:T(8,128)} %reshape.246) | data formatting | bytes 4194304 | tf_op jit(solution)/shard_map/reshape | solution.py:149
  420.8 11.7 %custom-call.11 = f32[16,8,8]{2,1,0:T(8,128)S(1)} custom-call(f32[16,8,8]{2,1,0:T(8,128)S(1)} %fusion.18), custom_call_target="Cholesky" | custom-call | tf_op jit(solution)/shard_map/jit(cholesky)/cholesky | solution.py:44
  432.8 10.0 %custom-call.12 = f32[16,1,8,8]{2,3,1,0:T(8,128)S(1)} custom-call(f32[16,1,8,8]{3,2,1,0:T(8,128)S(1)} %select_bitcast_fusion), custom_call_target="InvertDiagBlocksLowerTriangular" | custom-call | tf_op jit(solution)/shard_map/jit(_solve_triangular)/vmap()/triangular_solve | solution.py:46
  444.2 11.2 %fusion.56 = f32[256,64,8]{2,1,0:T(8,128)} fusion(f32[256,64,32]{2,1,0:T(8,128)} %reshape.246, f32[256,32,8]{1,2,0:T(8,128)S(1)} %copy.209), kind=kOutput, calls=%fused_computation.114 | convolution fusion | flops 50331648 | bytes 2883584 | tf_op jit(solution)/shard_map/scv,svk->sck/dot_general | solution.py:154
  455.4 7.4 %reshape.249 = f32[128,2,512]{2,1,0:T(2,128)} reshape(f32[256,64,8]{2,1,0:T(8,128)} %fusion.56) | data formatting | bytes 1048576 | tf_op jit(solution)/shard_map/reshape | solution.py:160
  462.8 6.3 %all-to-all-start.2 = ((f32[128,2,512]{2,1,0:T(2,128)}), f32[128,2,512]{2,1,0:T(2,128)S(1)}, u32[]{:S(2)}, u32[]{:S(2)}) async-start(f32[128,2,512]{2,1,0:T(2,128)} %reshape.249), calls=%async_computation.2 | async-start | bytes 1048576 | tf_op jit(solution)/shard_map/all_to_all | solution.py:101
  469.3 11.8 %all-to-all-done.2 = f32[128,2,512]{2,1,0:T(2,128)S(1)} async-done(((f32[128,2,512]{2,1,0:T(2,128)}), f32[128,2,512]{2,1,0:T(2,128)S(1)}, u32[]{:S(2)}, u32[]{:S(2)}) %all-to-all-start.2) | async-done | bytes 524320 | tf_op jit(solution)/shard_map/all_to_all | solution.py:101
  481.5 3.8 collective-permute-start.8
  487.4 4.6 collective-permute-done.9
  492.1 3.1 collective-permute-start.10
  495.1 2.7 collective-permute-start.11
  497.9 55.7 %copy.214 = f32[16,8,5,64,64]{4,3,2,1,0:T(8,128)} copy(f32[16,8,5,64,64]{0,1,4,3,2:T(8,128)} %bitcast) | data formatting | bytes 20971520 | tf_op jit(solution)/shard_map/reshape | solution.py:110
  553.7 4.5 reshape.244
  560.5 13.5 %gather.15 = f32[16,8,5,64,8]{4,3,2,1,0:T(8,128)} reshape(f32[640,512]{1,0:T(8,128)S(1)} %gather_fusion.1) | data formatting | bytes 2621440 | tf_op jit(solution)/shard_map/jit(_take)/gather | solution.py:60
  574.1 37.9 %fusion.4 = f32[16,8,5,64,8]{3,4,2,1,0:T(8,128)S(1)} fusion(f32[16,8,5,64,64]{4,3,2,1,0:T(8,128)} %copy.214, f32[16,8,5,64,8]{4,3,2,1,0:T(8,128)} %gather.15, pred[16,8,5]{2,1,0:T(8,128)(4,1)S(1)} %copy.211), kind=kOutput, calls=%fused_computation.16 | convolution fusion | flops 251985920 | bytes 13107840 | tf_op jit(solution)/shard_map/ijkoc,ijkcw->ijkow/dot_general | solution.py:167
  612.0 6.1 copy.215
  618.0 6.8 %copy.216 = f32[16,8,2560]{2,1,0:T(8,128)} copy(f32[16,8,2560]{0,2,1:T(8,128)} %bitcast.84) | data formatting | bytes 2621440
  (113 shorter events, 31.4 us)
Async XLA Ops:
  1.6 61.6 %collective-permute-start.1 = (f32[1,8,2048]{2,0,1:T(1,128)S(1)}, f32[1,8,2048]{2,0,1:T(1,128)S(1)}, u32[]{:S(2)}, u32[]{:S(2)}) collective-permute-start(f32[1,8,2048]{2,0,1:T(1,128)S(1)} %copy.174), channel_id=1, source_target_pairs={{8,0},{16,8},{24,16},{32,24},{40,32},{48,40},{56,48},{64,56},{72,6... | collective-permute-start | bytes 196616 | tf_op jit(solution)/shard_map/ppermute | solution.py:26
  4.1 59.0 %collective-permute-start = (f32[1,8,2048]{2,0,1:T(1,128)S(1)}, f32[1,8,2048]{2,0,1:T(1,128)S(1)}, u32[]{:S(2)}, u32[]{:S(2)}) collective-permute-start(f32[1,8,2048]{2,0,1:T(1,128)S(1)} %copy.173), channel_id=1, source_target_pairs={{0,8},{8,16},{16,24},{24,32},{32,40},{40,48},{48,56},{56,64},{64,7... | collective-permute-start | bytes 196616 | tf_op jit(solution)/shard_map/ppermute | solution.py:24
  11.6 39.3 %copy-start.4 = (s32[16,8,5]{2,1,0:T(8,128)}, s32[16,8,5]{2,1,0:T(8,128)S(1)}, u32[]{:S(2)}) copy-start(s32[16,8,5]{2,1,0:T(8,128)S(1)} %copy.172) | copy-start | bytes 7684
  11.9 39.0 %copy-start.7 = (s32[64]{0:T(128)}, s32[64]{0:T(128)S(1)}, u32[]{:S(2)}) copy-start(s32[64]{0:T(128)S(1)} %and_select_fusion.1) | copy-start | bytes 772
  50.9 11.7 %copy-start.2 = (f32[16,8,2048]{2,1,0:T(8,128)S(1)}, f32[16,8,2048]{2,1,0:T(8,128)}, u32[]{:S(2)}) copy-start(f32[16,8,2048]{2,1,0:T(8,128)} %param.9) | copy-start | bytes 3145732
  63.2 82.5 %collective-permute-start.2 = (f32[18,1,2048]{2,0,1:T(8,128)S(1)}, f32[18,1,2048]{2,0,1:T(8,128)S(1)}, u32[]{:S(2)}, u32[]{:S(2)}) collective-permute-start(f32[18,1,2048]{2,0,1:T(8,128)S(1)} %get-tuple-element.25), channel_id=1, source_target_pairs={{0,1},{1,2},{2,3},{3,4},{4,5},{5,6},{6,7},{8,9},{9,10},{10,11},{11... | collective-permute-start | bytes 442376 | tf_op jit(solution)/shard_map/ppermute | solution.py:24
  67.6 78.2 %collective-permute-start.3 = (f32[18,1,2048]{2,0,1:T(8,128)S(1)}, f32[18,1,2048]{2,0,1:T(8,128)S(1)}, u32[]{:S(2)}, u32[]{:S(2)}) collective-permute-start(f32[18,1,2048]{2,0,1:T(8,128)S(1)} %get-tuple-element.26), channel_id=1, source_target_pairs={{1,0},{2,1},{3,2},{4,3},{5,4},{6,5},{7,6},{9,8},{10,9},{11,10},{12... | collective-permute-start | bytes 442376 | tf_op jit(solution)/shard_map/ppermute | solution.py:26
  211.1 5.2 copy-start
  211.4 12.2 %collective-permute-start.4 = (f32[1,8,2048]{2,1,0:T(8,128)S(1)}, f32[1,8,2048]{2,1,0:T(8,128)S(1)}, u32[]{:S(2)}, u32[]{:S(2)}) collective-permute-start(f32[1,8,2048]{2,1,0:T(8,128)S(1)} %slice.78), channel_id=1, source_target_pairs={{0,8},{8,16},{16,24},{24,32},{32,40},{40,48},{48,56},{56,64},{64,7... | collective-permute-start | bytes 196616 | tf_op jit(solution)/shard_map/ppermute | solution.py:24
  216.5 7.1 %collective-permute-start.5 = (f32[1,8,2048]{2,1,0:T(8,128)S(1)}, f32[1,8,2048]{2,1,0:T(8,128)S(1)}, u32[]{:S(2)}, u32[]{:S(2)}) collective-permute-start(f32[1,8,2048]{2,1,0:T(8,128)S(1)} %slice.80), channel_id=1, source_target_pairs={{8,0},{16,8},{24,16},{32,24},{40,32},{48,40},{56,48},{64,56},{72,6... | collective-permute-start | bytes 196616 | tf_op jit(solution)/shard_map/ppermute | solution.py:26
  223.9 18.2 %collective-permute-start.6 = (f32[18,1,2048]{2,1,0:T(1,128)S(1)}, f32[18,1,2048]{2,1,0:T(1,128)S(1)}, u32[]{:S(2)}, u32[]{:S(2)}) collective-permute-start(f32[18,1,2048]{2,1,0:T(1,128)S(1)} %get-tuple-element.23), channel_id=1, source_target_pairs={{0,1},{1,2},{2,3},{3,4},{4,5},{5,6},{6,7},{8,9},{9,10},{10,11},{11... | collective-permute-start | bytes 442376 | tf_op jit(solution)/shard_map/ppermute | solution.py:24
  228.6 13.5 %collective-permute-start.7 = (f32[18,1,2048]{2,1,0:T(1,128)S(1)}, f32[18,1,2048]{2,1,0:T(1,128)S(1)}, u32[]{:S(2)}, u32[]{:S(2)}) collective-permute-start(f32[18,1,2048]{2,1,0:T(1,128)S(1)} %get-tuple-element.24), channel_id=1, source_target_pairs={{1,0},{2,1},{3,2},{4,3},{5,4},{6,5},{7,6},{9,8},{10,9},{11,10},{12... | collective-permute-start | bytes 442376 | tf_op jit(solution)/shard_map/ppermute | solution.py:26
  231.3 133.9 %all-to-all-start.1 = ((s32[128,1,2]{2,1,0:T(1,128)}), s32[128,1,2]{2,1,0:T(1,128)S(1)}, u32[]{:S(2)}, u32[]{:S(2)}) async-start(s32[128,1,2]{2,1,0:T(1,128)} %copy.196), calls=%async_computation.1 | async-start | bytes 131072 | tf_op jit(solution)/shard_map/all_to_all | solution.py:95
  255.4 13.8 %copy-start.1 = (f32[16,8,64,32]{2,3,1,0:T(8,128)S(1)}, f32[16,8,64,32]{2,3,1,0:T(8,128)}, u32[]{:S(2)}) copy-start(f32[16,8,64,32]{2,3,1,0:T(8,128)} %copy-done) | copy-start | bytes 3145732
  357.6 3.5 copy-start.8
  365.2 41.0 %all-to-all-start = ((f32[128,2,2048]{2,1,0:T(2,128)}), f32[128,2,2048]{2,1,0:T(2,128)S(1)}, u32[]{:S(2)}, u32[]{:S(2)}) async-start(f32[128,2,2048]{2,1,0:T(2,128)} %copy.192), calls=%async_computation | async-start | bytes 4194304 | tf_op jit(solution)/shard_map/all_to_all | solution.py:94
  455.4 13.7 %copy-start.5 = (s32[16,8,5]{2,1,0:T(8,128)S(1)}, s32[16,8,5]{2,1,0:T(8,128)}, u32[]{:S(2)}) copy-start(s32[16,8,5]{2,1,0:T(8,128)} %copy-done.4) | copy-start | bytes 7684
  462.8 18.3 %all-to-all-start.2 = ((f32[128,2,512]{2,1,0:T(2,128)}), f32[128,2,512]{2,1,0:T(2,128)S(1)}, u32[]{:S(2)}, u32[]{:S(2)}) async-start(f32[128,2,512]{2,1,0:T(2,128)} %reshape.249), calls=%async_computation.2 | async-start | bytes 1048576 | tf_op jit(solution)/shard_map/all_to_all | solution.py:101
  481.5 5.8 collective-permute-start.8
  485.4 68.2 %copy-start.3 = (f32[16,8,512]{2,1,0:T(8,128)}, f32[16,8,512]{2,1,0:T(8,128)S(1)}, u32[]{:S(2)}) copy-start(f32[16,8,512]{2,1,0:T(8,128)S(1)} %reshape_reshape_reshape.7) | copy-start | bytes 786436
  485.4 6.6 %collective-permute-start.9 = (f32[1,8,512]{2,1,0:T(8,128)S(1)}, f32[1,8,512]{2,1,0:T(8,128)S(1)}, u32[]{:S(2)}, u32[]{:S(2)}) collective-permute-start(f32[1,8,512]{2,1,0:T(8,128)S(1)} %slice.87), channel_id=1, source_target_pairs={{8,0},{16,8},{24,16},{32,24},{40,32},{48,40},{56,48},{64,56},{72,6... | collective-permute-start | bytes 49160 | tf_op jit(solution)/shard_map/ppermute | solution.py:26
  492.1 66.1 %collective-permute-start.10 = (f32[18,1,512]{2,1,0:T(1,128)S(1)}, f32[18,1,512]{2,1,0:T(1,128)S(1)}, u32[]{:S(2)}, u32[]{:S(2)}) collective-permute-start(f32[18,1,512]{2,1,0:T(1,128)S(1)} %get-tuple-element.29), channel_id=1, source_target_pairs={{0,1},{1,2},{2,3},{3,4},{4,5},{5,6},{6,7},{8,9},{9,10},{10,11},{11... | collective-permute-start | bytes 110600 | tf_op jit(solution)/shard_map/ppermute | solution.py:24
  495.1 63.0 %collective-permute-start.11 = (f32[18,1,512]{2,1,0:T(1,128)S(1)}, f32[18,1,512]{2,1,0:T(1,128)S(1)}, u32[]{:S(2)}, u32[]{:S(2)}) collective-permute-start(f32[18,1,512]{2,1,0:T(1,128)S(1)} %get-tuple-element.30), channel_id=1, source_target_pairs={{1,0},{2,1},{3,2},{4,3},{5,4},{6,5},{7,6},{9,8},{10,9},{11,10},{12... | collective-permute-start | bytes 110600 | tf_op jit(solution)/shard_map/ppermute | solution.py:26
  497.9 55.7 %copy-start.6 = (pred[16,8,5]{0,1,2:T(8,128)(4,1)S(1)}, pred[16,8,5]{0,1,2:T(8,128)(4,1)}, u32[]{:S(2)}) copy-start(pred[16,8,5]{0,1,2:T(8,128)(4,1)} %get-tuple-element.19) | copy-start | bytes 1924
